TPU v7x, 32 devices: a whole 2x2x4 slice. The times are simulated.
32 devices in a mesh: dp: 16 (over z, x, core), tensor: 2 (over y).
Axes of the slice: x: 2, y: 2, z: 4, core: 2. Of those that a mesh axis runs over, the one named last changes fastest.
Arguments:
- x_in: bfloat16 [16384, 2048], P('dp'), may hold values from -6 to 6
- norm_gain: float32 [2048], replicated, may hold values from 0.5 to 1.5
- w_zx: bfloat16 [2048, 2, 4096], P(None, None, 'tensor'), may hold values from -0.125 to 0.125
- w_bc: bfloat16 [2048, 256], replicated, may hold values from -0.125 to 0.125
- w_dt: bfloat16 [2048, 64], P(None, 'tensor'), may hold values from -0.125 to 0.125
- conv_x: float32 [5, 4096], P(None, 'tensor'), may hold values from -3 to 3
- conv_bc: float32 [5, 256], replicated, may hold values from -3 to 3
- dt_bias: float32 [64], P('tensor'), may hold values from -4 to -1
- a_log: float32 [64], P('tensor'), may hold values from -3 to 1.5
- d_skip: float32 [64], P('tensor'), may hold values from 0.5 to 1.5
- gate_gain: float32 [4096], P('tensor'), may hold values from 0.5 to 1.5
- w_out: bfloat16 [4096, 2048], P('tensor'), may hold values from -0.09375 to 0.09375
- cotangent: bfloat16 [16384, 2048], P('dp'), may hold values from -6 to 6
- block_parent: int32 [128], P('dp'), may hold values from -1 to 6, as said below
Outputs:
- mixed: bfloat16 [16384, 2048], P('dp')
- input_grad: bfloat16 [16384, 2048], P('dp')
- norm_gain_grad: float32 [2048], replicated
- w_zx_grad: float32 [2048, 2, 4096], P('dp', None, 'tensor')
- w_bc_grad: float32 [2048, 256], replicated
- w_dt_grad: float32 [2048, 64], P('dp', 'tensor')
- conv_x_grad: float32 [5, 4096], P(None, 'tensor')
- conv_bc_grad: float32 [5, 256], replicated
- dt_bias_grad: float32 [64], P('tensor')
- a_log_grad: float32 [64], P('tensor')
- d_skip_grad: float32 [64], P('tensor')
- gate_gain_grad: float32 [4096], P('tensor')
- w_out_grad: float32 [4096, 2048], P('tensor', 'dp')
Inputs may be any that keep to these rules, and one draw needn't show every extreme that they name: `block_parent`: each device's 8 blocks hold one tree. A block's entry is the index, among its device's blocks, of an earlier block whose last token precedes its first token, or -1 at the root; the first half of the blocks or more form a chain from the root, and the last block continues the block before it.
All inputs are finite; a program needn't handle non-finite values.
Results may differ from a plain program's by a relative error of at most 0.014.
Values may be sent and summed in bfloat16 or wider, within the bound.
No kernel may reach another device: no remote copies, remote signals or barrier semaphores. Data moves between devices by JAX's collectives and lax.ppermute only.
A program may use at most 320 MiB of HBM per device.

v0:
```python
import jax
import jax.numpy as jnp
from jax import lax
from jax.sharding import PartitionSpec as P

epsilon = 1e-05
highest = lax.Precision.HIGHEST


def conv_path(inputs, kernel, parent):
    blocks = parent.shape[0]
    tokens, channels = inputs.shape
    window = kernel.shape[0] - 1
    block_len = tokens // blocks
    blocked = inputs.reshape(blocks, block_len, channels)
    trailing = blocked[:, block_len - (window - 1) :, :]
    context = jnp.take(trailing, jnp.maximum(parent, 0), axis=0)
    context = jnp.where((parent >= 0)[:, None, None], context, jnp.zeros_like(context))
    padded = jnp.concatenate([context, blocked], axis=1)
    summed = kernel[window][None, None, :] + jnp.zeros_like(blocked)
    for offset in range(window):
        summed = summed + kernel[offset][None, None, :] * padded[:, offset : offset + block_len, :]
    return jax.nn.silu(summed).reshape(tokens, channels)


def decay_paths(block_decay, parent):
    blocks = parent.shape[0]
    n_heads = block_decay.shape[1]
    parent_map = (parent[:, None] == jnp.arange(blocks, dtype=jnp.int32)[None, :]).astype(
        jnp.float32
    )
    identity = jnp.eye(blocks, dtype=jnp.float32)

    def advance(turn, paths):
        return identity[None] + jnp.einsum(
            "hb,bp,hpa->hba", block_decay.T, parent_map, paths, precision=highest
        )

    paths = lax.fori_loop(0, blocks, advance, jnp.broadcast_to(identity, (n_heads, blocks, blocks)))
    return (paths, parent_map)


def ssd_mix(x_heads, b_rows, c_rows, dt_raw, dt_bias, a_log, d_skip, parent):
    tokens, n_heads, head_dim = x_heads.shape
    blocks = parent.shape[0]
    block_len = tokens // blocks
    dt_values = jax.nn.softplus(dt_raw + dt_bias)
    log_rate = dt_values * -jnp.exp(a_log)
    x_blocks = x_heads.reshape(blocks, block_len, n_heads, head_dim)
    b_blocks = b_rows.reshape(blocks, block_len, -1)
    c_blocks = c_rows.reshape(blocks, block_len, -1)
    dt_blocks = dt_values.reshape(blocks, block_len, n_heads)
    cumulant = jnp.cumsum(log_rate.reshape(blocks, block_len, n_heads), axis=1)
    scores = jnp.einsum("bin,bjn->bij", c_blocks, b_blocks, precision=highest)
    rows_idx = jnp.arange(block_len, dtype=jnp.int32)
    causal = (rows_idx[:, None] >= rows_idx[None, :])[None, :, :, None]
    log_gap = cumulant[:, :, None, :] - cumulant[:, None, :, :]
    decays = jnp.where(causal, jnp.exp(jnp.where(causal, log_gap, 0.0)), 0.0)
    weights = scores[..., None] * decays * dt_blocks[:, None, :, :]
    within = jnp.einsum("bijh,bjhp->bihp", weights, x_blocks, precision=highest)
    to_end = jnp.exp(cumulant[:, -1:, :] - cumulant) * dt_blocks
    local_states = jnp.einsum("bjh,bjhp,bjn->bhpn", to_end, x_blocks, b_blocks, precision=highest)
    paths, parent_map = decay_paths(jnp.exp(cumulant[:, -1, :]), parent)
    end_states = jnp.einsum("hba,ahpn->bhpn", paths, local_states, precision=highest)
    start_states = jnp.einsum("bq,qhpn->bhpn", parent_map, end_states, precision=highest)
    carried = jnp.exp(cumulant)[..., None] * jnp.einsum(
        "bin,bhpn->bihp", c_blocks, start_states, precision=highest
    )
    result = within + carried + d_skip[None, None, :, None] * x_blocks
    return result.reshape(tokens, n_heads * head_dim)


def gated_mix(x_heads, bc_rows, dt_raw, dt_bias, a_log, d_skip, z_gate, parent):
    half = bc_rows.shape[1] // 2
    mixed_heads = ssd_mix(
        x_heads, bc_rows[:, :half], bc_rows[:, half:], dt_raw, dt_bias, a_log, d_skip, parent
    )
    return mixed_heads * jax.nn.silu(z_gate)


def over_tokens(left, right):
    return lax.dot_general(
        left, right, (((0,), (0,)), ((), ())), preferred_element_type=jnp.float32
    )


def over_columns(left, right):
    return lax.dot_general(
        left, right, (((1,), (1,)), ((), ())), preferred_element_type=jnp.float32
    )


def rounded(value):
    return lax.optimization_barrier(value.astype(jnp.bfloat16)).astype(jnp.float32)


def local(
    x_in,
    norm_gain,
    w_zx,
    w_bc,
    w_dt,
    conv_x,
    conv_bc,
    dt_bias,
    a_log,
    d_skip,
    gate_gain,
    w_out,
    cotangent,
    block_parent,
):
    tokens, features = x_in.shape
    local_heads = w_dt.shape[1]
    inner_width = w_zx.shape[2]
    head_dim = inner_width // local_heads
    full_width = inner_width * lax.axis_size("tensor")
    x_float = x_in.astype(jnp.float32)
    inv_rms = lax.rsqrt(jnp.mean(x_float * x_float, axis=-1) + epsilon)
    normed = (x_float * inv_rms[:, None] * norm_gain).astype(jnp.bfloat16)
    z_gate = jnp.dot(normed, w_zx[:, 0, :], preferred_element_type=jnp.float32)
    x_pre = jnp.dot(normed, w_zx[:, 1, :], preferred_element_type=jnp.float32)
    bc_pre = jnp.dot(normed, w_bc, preferred_element_type=jnp.float32)
    dt_raw = jnp.dot(normed, w_dt, preferred_element_type=jnp.float32)

    def x_piece(values, kernel):
        return conv_path(values, kernel, block_parent)

    x_conv, x_pull = jax.vjp(x_piece, x_pre, conv_x)
    bc_conv, bc_pull = jax.vjp(x_piece, bc_pre, conv_bc)
    x_round = rounded(x_conv)
    bc_round = rounded(bc_conv)

    def mixer(x_values, bc_values, dt_values, bias_values, log_values, skip_values, gate_values):
        return gated_mix(
            x_values.reshape(tokens, local_heads, head_dim),
            bc_values,
            dt_values,
            bias_values,
            log_values,
            skip_values,
            gate_values,
            block_parent,
        )

    gated, mix_pull = jax.vjp(mixer, x_round, bc_round, dt_raw, dt_bias, a_log, d_skip, z_gate)
    squares = lax.psum(jnp.sum(gated * gated, axis=-1), "tensor")
    inv_gate = lax.rsqrt(squares / full_width + epsilon)
    gate_normed = (gated * inv_gate[:, None] * gate_gain).astype(jnp.bfloat16)
    partial_out = jnp.dot(gate_normed, w_out, preferred_element_type=jnp.float32)
    share = tokens // lax.axis_size("tensor")
    first_row = lax.axis_index("tensor") * share
    x_rows = lax.dynamic_slice_in_dim(x_float, first_row, share, 0)
    mixed = (
        x_float + lax.psum(partial_out.astype(jnp.bfloat16), "tensor").astype(jnp.float32)
    ).astype(jnp.bfloat16)
    d_gate_normed = over_columns(cotangent, w_out)
    w_out_part = over_tokens(gate_normed, cotangent)
    gate_gain_part = jnp.sum(d_gate_normed * gated * inv_gate[:, None], axis=0)
    scaled = d_gate_normed * gate_gain
    cross = lax.psum(jnp.sum(scaled * gated, axis=-1), "tensor")
    d_gated = (
        inv_gate[:, None] * scaled
        - gated * (inv_gate * inv_gate * inv_gate * cross / full_width)[:, None]
    )
    d_x_round, d_bc_round, d_dt_raw, dt_bias_part, a_log_part, d_skip_part, d_z_gate = mix_pull(
        d_gated
    )
    d_x_pre, conv_x_part = x_pull(d_x_round)
    d_bc_pre, conv_bc_part = bc_pull(d_bc_round)
    z_low = d_z_gate.astype(jnp.bfloat16)
    x_low = d_x_pre.astype(jnp.bfloat16)
    bc_low = d_bc_pre.astype(jnp.bfloat16)
    dt_low = d_dt_raw.astype(jnp.bfloat16)
    w_zx_part = jnp.stack([over_tokens(normed, z_low), over_tokens(normed, x_low)], axis=1)
    w_bc_part = over_tokens(normed, bc_low)
    w_dt_part = over_tokens(normed, dt_low)
    d_normed = over_columns(z_low, w_zx[:, 0, :]) + over_columns(x_low, w_zx[:, 1, :])
    d_normed = d_normed + over_columns(bc_low, w_bc) + over_columns(dt_low, w_dt)
    norm_gain_part = jnp.sum(d_normed * x_float * inv_rms[:, None], axis=0)
    d_rows = lax.psum_scatter(
        d_normed.astype(jnp.bfloat16), "tensor", scatter_dimension=0, tiled=True
    ).astype(jnp.float32)
    rms_rows = lax.dynamic_slice_in_dim(inv_rms, first_row, share, 0)
    cot_rows = lax.dynamic_slice_in_dim(cotangent, first_row, share, 0).astype(jnp.float32)
    gained = d_rows * norm_gain
    spread = rms_rows * rms_rows * rms_rows * jnp.sum(gained * x_rows, axis=-1) / features
    d_input = cot_rows + rms_rows[:, None] * gained - x_rows * spread[:, None]
    input_grad = lax.all_gather(d_input.astype(jnp.bfloat16), "tensor", axis=0, tiled=True)
    w_zx_grad, w_dt_grad, w_out_grad = (
        lax.psum_scatter(
            w_zx_part.astype(jnp.bfloat16), "dp", scatter_dimension=0, tiled=True
        ).astype(jnp.float32),
        lax.psum_scatter(
            w_dt_part.astype(jnp.bfloat16), "dp", scatter_dimension=0, tiled=True
        ).astype(jnp.float32),
        lax.psum_scatter(
            w_out_part.astype(jnp.bfloat16), "dp", scatter_dimension=1, tiled=True
        ).astype(jnp.float32),
    )
    conv_x_grad, dt_bias_grad, a_log_grad, d_skip_grad, gate_gain_grad = lax.psum(
        (conv_x_part, dt_bias_part, a_log_part, d_skip_part, gate_gain_part), "dp"
    )
    norm_gain_grad, w_bc_grad, conv_bc_grad = lax.psum(
        (norm_gain_part, w_bc_part, conv_bc_part), ("dp", "tensor")
    )
    return (
        mixed,
        input_grad,
        norm_gain_grad,
        w_zx_grad,
        w_bc_grad,
        w_dt_grad,
        conv_x_grad,
        conv_bc_grad,
        dt_bias_grad,
        a_log_grad,
        d_skip_grad,
        gate_gain_grad,
        w_out_grad,
    )


def solution(mesh):
    return jax.shard_map(
        local,
        mesh=mesh,
        in_specs=(
            P("dp", None),
            P(),
            P(None, None, "tensor"),
            P(),
            P(None, "tensor"),
            P(None, "tensor"),
            P(),
            P("tensor"),
            P("tensor"),
            P("tensor"),
            P("tensor"),
            P("tensor", None),
            P("dp", None),
            P("dp"),
        ),
        out_specs=(
            P("dp", None),
            P("dp", None),
            P(),
            P("dp", None, "tensor"),
            P(),
            P("dp", "tensor"),
            P(None, "tensor"),
            P(),
            P("tensor"),
            P("tensor"),
            P("tensor"),
            P("tensor"),
            P("tensor", "dp"),
        ),
        check_vma=False,
    )
```

profile of v0, /device:TPU:0, one launch (start us, length us, event | category | flops | bytes accessed | tf_op | source)
XLA Modules:
  0.0 1176.5 jit_solution(15319442505596880165)
XLA Ops:
  12.6 32.8 %fusion.165 = (bf16[2048,1,2048]{2,1,0:T(2,128)(2,1)}, bf16[2048,1,2048]{2,1,0:T(2,128)(2,1)}) fusion(bf16[2048,2,2048]{2,1,0:T(2,128)(2,1)} %param.20), kind=kLoop, calls=%fused_computation.254 | loop fusion | bytes 33554432 | tf_op jit(solution)/shard_map/slice | solution.py:121
  64.3 16.3 %multiply_convert_fusion.1 = (bf16[8,128,2048]{2,1,0:T(8,128)(2,1)}, f32[8,128,2048]{2,1,0:T(8,128)}) fusion(f32[8,128,2048]{2,1,0:T(8,128)} %copy-done.7, f32[2048]{0:T(1024)S(1)} %bitcast.305, f32[8,3,2048]{2,1,0:T(4,128)S(1)} %select_select_fusion, f32[2048]{0:T(1024)S(1)} %bitcast.307, f32[2048]{0:T(1024)S(1)} %bitcast.301, f32[2048]{0:T(1024)S(1)} %bitcast.303, ...), kind=kLoop, calls=%fused_computation.101 | loop fusion | flops 33554432 | bytes 21209088 | tf_op jit(solution)/shard_map/convert_element_type | solution.py:94
  104.8 23.3 %fusion.171 = f32[8,128,32]{2,0,1:T(8,128)S(1)} fusion(f32[8,128,32]{2,0,1:T(8,128)S(1)} %copy.143), kind=kOutput, calls=%fused_computation.260 | output fusion | flops 4161536 | bytes 262144 | tf_op jit(solution)/shard_map/jvp(jit(cumsum))/reduce_window_sum | solution.py:53
  211.3 21.9 %fusion.39 = f32[8,128,32,64]{1,3,2,0:T(8,128)} fusion(f32[8,128,32,64]{1,3,2,0:T(8,128)} %copy.158, f32[8,128,32,64]{1,3,2,0:T(8,128)S(1)} %fusion.69, f32[32]{0:T(128)S(1)} %copy-done.90, f32[8,128,32]{1,2,0:T(8,128)S(1)} %copy.148, f32[8,128,32]{1,2,0:T(8,128)S(1)} %bitcast.298, f32[8,128,32]{1,2,0:T(8,128)S(1)} %copy-done.36, ...), kind=kOutput, calls=%fused_computation.62 | convolution fusion | flops 3250585600 | bytes 30294144 | tf_op jit(solution)/shard_map/jvp(bijh,bjhp->bihp)/dot_general | solution.py:60
  233.2 16.2 %copy.215 = f32[8,128,32,64]{3,2,1,0:T(8,128)} copy(f32[8,128,32,64]{1,3,2,0:T(8,128)} %fusion.39) | data formatting | bytes 16777216 | tf_op jit(solution)/shard_map/jvp()/reshape | solution.py:70
  264.3 19.7 %multiply_reduce_fusion.11 = (f32[1024]{0:T(1024)S(1)}, f32[1024,2048]{1,0:T(8,128)}, f32[1024,2048]{1,0:T(8,128)}) fusion(f32[1024,2048]{1,0:T(8,128)} %reshape.284, bf16[1024,2048]{1,0:T(8,128)(2,1)} %copy-done.2, bf16[2048,1,2048]{2,1,0:T(2,128)(2,1)} %get-tuple-element.379), kind=kOutput, calls=%fused_computation.85 | convolution fusion | flops 8604613632 | bytes 37752832 | tf_op jit(solution)/shard_map/dot_general | solution.py:121
  289.9 15.3 %convolution_convert_fusion.1 = bf16[1024,2048]{1,0:T(8,128)(2,1)} fusion(bf16[2048,2048]{1,0:T(8,128)(2,1)} %param.29, f32[1024,2048]{1,0:T(8,128)} %get-tuple-element.373, f32[2048]{0:T(1024)S(1)} %copy-done.73, f32[1024]{0:T(1024)S(1)} %add_rsqrt_fusion), kind=kOutput, calls=%fused_computation.140 | convolution fusion | flops 8598323200 | bytes 20983808 | tf_op jit(solution)/shard_map/dot_general | solution.py:150
  305.2 17.0 %multiply_reduce_fusion.2 = (f32[2048]{0:T(1024)}, f32[1024]{0:T(1024)S(1)}, f32[1024,2048]{1,0:T(8,128)}) fusion(f32[1024,2048]{1,0:T(8,128)} %get-tuple-element.373, f32[1024]{0:T(1024)S(1)} %add_rsqrt_fusion, f32[2048]{0:T(1024)S(1)} %copy-done.73, bf16[1024,2048]{1,0:T(8,128)(2,1)} %param.30, bf16[2048,2048]{1,0:T(8,128)(2,1)} %param.29), kind=kOutput, calls=%fused_computation.70 | convolution fusion | flops 8602514432 | bytes 29384704 | tf_op jit(solution)/shard_map/dot_general | solution.py:88
  327.2 20.5 %multiply_reduce_fusion.3 = (f32[2048]{0:T(1024)}, f32[1024,2048]{1,0:T(8,128)}, bf16[1024,2048]{1,0:T(8,128)(2,1)}) fusion(bf16[1024,2048]{1,0:T(8,128)(2,1)} %bitcast.262, f32[1024,2048]{1,0:T(8,128)} %get-tuple-element.413, f32[1024,2048]{1,0:T(8,128)} %get-tuple-element.373, f32[1024]{0:T(1024)S(1)} %fusion.141, f32[1024,2048]{1,0:T(8,128)} %get-tuple-element.414, ...), kind=kLoop, calls=%fused_computation.71 | loop fusion | flops 41940992 | bytes 50356224 | tf_op jit(solution)/shard_map/transpose(jvp())/reduce_sum | solution.py:69
  391.1 21.3 %fusion.106 = f32[32,8,8]{2,1,0:T(8,128)S(1)} fusion(f32[32,64,128,8]{2,3,1,0:T(8,128)S(1)} %fusion.44, f32[8,32,64,128]{3,2,1,0:T(8,128)S(1)} %bitcast.259), kind=kOutput, calls=%fused_computation.159 | convolution fusion | flops 201326592 | bytes 16785408 | tf_op jit(solution)/shard_map/transpose(jvp(hba,ahpn->bhpn))/dot_general | solution.py:64
  429.7 18.2 %fusion.103 = f32[8,128,128]{2,1,0:T(8,128)S(1)} fusion(f32[8,32,64,128]{3,0,2,1:T(8,128)} %convolution_bitcast_fusion.1, f32[8,128,32]{1,2,0:T(8,128)S(1)} %copy-done.29, bf16[8,128,32,64]{1,0,3,2:T(8,128)(2,1)S(1)} %bitcast.266), kind=kOutput, calls=%fused_computation.156 | convolution fusion | flops 3225419776 | bytes 13238272 | tf_op jit(solution)/shard_map/transpose(jvp(bjh,bjhp,bjn->bhpn))/dot_general | solution.py:62
  448.0 15.7 %fusion.98 = f32[8,128,128]{2,1,0:T(8,128)S(1)} fusion(f32[8,32,64,128]{3,0,2,1:T(8,128)S(1)} %bitcast.257, f32[8,128,32,64]{1,0,3,2:T(8,128)S(1)} %bitcast.252, f32[8,128,32]{1,2,0:T(8,128)S(1)} %copy.148), kind=kOutput, calls=%fused_computation.155 | convolution fusion | flops 3223322624 | bytes 17432576 | tf_op jit(solution)/shard_map/transpose(jvp(bin,bhpn->bihp))/dot_general | solution.py:66
  463.8 28.9 %fusion.28 = (f32[8,128,32]{1,2,0:T(8,128)}, f32[8,128,32]{1,2,0:T(8,128)S(1)}, f32[8,128,32]{1,2,0:T(8,128)}, f32[8,128,128]{2,1,0:T(8,128)S(1)}) fusion(f32[8,128,32]{1,2,0:T(8,128)S(1)} %bitcast.299, f32[8,128,32]{1,2,0:T(8,128)S(1)} %copy-done.37, f32[8,128,128]{2,1,0:T(8,128)S(1)} %copy-done.31, pred[128,128]{1,0:T(8,128)(4,1)S(1)} %copy-done.64, ...), kind=kOutput, calls=%fused_computation.44 | convolution fusion | flops 3283910656 | bytes 14303232 | tf_op jit(solution)/shard_map/transpose(jvp(bijh,bjhp->bihp))/dot_general | solution.py:60
  508.4 23.6 %bitcast_add_fusion = f32[8,128,32,64]{1,3,2,0:T(8,128)} fusion(f32[8,128,32,64]{1,3,2,0:T(8,128)} %fusion.65, f32[8,128,32,64]{1,0,3,2:T(8,128)S(1)} %bitcast.255, f32[32]{0:T(128)S(1)} %copy-done.91, f32[8,128,32]{1,2,0:T(8,128)S(1)} %copy-done.29, f32[8,128,32]{1,2,0:T(8,128)S(1)} %bitcast.300, f32[8,128,32]{1,2,0:T(8,128)S(1)} %copy-done.37, ...), kind=kOutput, calls=%fused_computation.58 | convolution fusion | flops 3250585600 | bytes 34488448 | tf_op jit(solution)/shard_map/transpose(jvp(bijh,bjhp->bihp))/dot_general | solution.py:60
  536.4 36.3 %while.31 = (s32[]{:T(128)}, f32[8,32]{1,0:T(8,128)}, f32[32,8,8]{2,1,0:T(8,128)S(1)}, f32[8,32,8,8]{3,2,1,0:T(8,128)}, s32[8]{0:T(128)}, /*index=5*/f32[8,32]{0...) while((s32[]{:T(128)}, f32[8,32]{1,0:T(8,128)}, f32[32,8,8]{2,1,0:T(8,128)S(1)}, ...), condition=%wide.region_15.16_spmd.clone, body=%wide.region_14.15_spmd.clone.sunk | while | flops 420484 | bytes 210855 | solution.py:39
  590.6 18.6 %multiply_reduce_fusion.6 = (f32[2048]{0:T(1024)}, f32[2048]{0:T(1024)}, f32[2048]{0:T(1024)}, f32[2048]{0:T(1024)}, f32[2048]{0:T(1024)}, /*index=5*/f32[8,128,2048]{2,1,0:T(8,128)S(1)}) fusion(f32[8,128,2048]{2,1,0:T(8,128)} %copy-done.7, f32[8,3,2048]{2,1,0:T(4,128)S(1)} %copy-done.19, f32[8,128,2048]{2,1,0:T(8,128)} %get-tuple-element.377, ...), kind=kLoop, calls=%fused_computation.74 | loop fusion | flops 44029952 | bytes 33792000 | tf_op jit(solution)/shard_map/transpose(jvp())/reduce_sum | solution.py:22
  650.6 15.6 %fusion.87 = f32[1024,2048]{1,0:T(8,128)} fusion(bf16[1024,2048]{1,0:T(8,128)(2,1)S(1)} %copy-done.15, bf16[2048,1,2048]{2,1,0:T(2,128)(2,1)} %get-tuple-element.379), kind=kOutput, calls=%fused_computation.142 | convolution fusion | flops 8589934592 | bytes 20971520 | tf_op jit(solution)/shard_map/dot_general | solution.py:88
  666.2 24.1 %multiply_reduce_fusion.8 = (f32[2048]{0:T(1024)S(1)}, bf16[1024,2048]{1,0:T(8,128)(2,1)}, bf16[1024,2048]{1,0:T(8,128)(2,1)}) fusion(bf16[1024,2048]{1,0:T(8,128)(2,1)} %param.18, f32[1024]{0:T(1024)S(1)} %copy-done.59, bf16[1024,2048]{1,0:T(8,128)(2,1)} %all-reduce.29.cloned.1.call-done, f32[1024,2048]{1,0:T(8,128)} %fusion.138, ...), kind=kOutput, calls=%fused_computation.78 | convolution fusion | flops 8613001216 | bytes 54538240 | tf_op jit(solution)/shard_map/dot_general | solution.py:88
  728.9 17.5 %reduce-scatter.9.cloned.1.call-done = bf16[512,2048]{1,0:T(8,128)(2,1)} async-done(((bf16[1024,2048]{1,0:T(8,128)(2,1)}), bf16[512,2048]{1,0:T(8,128)(2,1)}) %reduce-scatter.9.cloned.1.call-update) | async-done | bytes 2097168 | tf_op jit(solution)/shard_map/reduce_scatter | solution.py:181
  790.7 63.7 %all-reduce.25 = (f32[5,2048]{1,0:T(8,128)}, f32[32]{0:T(128)}, f32[32]{0:T(128)}, f32[32]{0:T(128)}, f32[2048]{0:T(1024)}) all-reduce(f32[5,2048]{1,0:T(8,128)S(1)} %pad_add_fusion.3, f32[32]{0:T(128)S(1)} %get-tuple-element.364, f32[32]{0:T(128)S(1)} %negate_multiply_fusion, ...), channel_id=1, replica_groups=mesh['dp'=16,'tensor'=2] {'dp'}, use_global_device_ids=true, to_apply=%region_32.33 | all-reduce | flops 12384 | bytes 99072 | tf_op jit(solution)/shard_map/psum | solution.py:201
  855.9 39.0 %all-reduce.24 = (f32[2048]{0:T(1024)}, f32[5,256]{1,0:T(8,128)}) all-reduce(f32[2048]{0:T(1024)S(1)} %get-tuple-element.381, f32[5,256]{1,0:T(8,128)S(1)} %pad_add_fusion.4), channel_id=1, replica_groups=mesh['dp'=16,'tensor'=2] {'dp','tensor'}, use_global_device_ids=true, to_apply=%region_23.24 | all-reduce | flops 3328 | bytes 26624 | tf_op jit(solution)/shard_map/psum | solution.py:204
  894.8 22.0 %reduce-scatter.15.cloned.1.call-done = bf16[128,2048]{1,0:T(8,128)(2,1)} async-done(((bf16[2048,2048]{1,0:T(8,128)(2,1)}), bf16[128,2048]{1,0:T(8,128)(2,1)}) %reduce-scatter.15.cloned.1.call-update) | async-done | bytes 524304
  919.2 56.4 %all-gather.2.cloned.1.call-done = bf16[1024,2048]{1,0:T(8,128)(2,1)} async-done(((bf16[512,2048]{1,0:T(8,128)(2,1)}), bf16[1024,2048]{1,0:T(8,128)(2,1)}) %all-gather.2.cloned.1.call-update) | async-done | bytes 4194320 | tf_op jit(solution)/shard_map/all_gather | solution.py:189
  975.6 183.1 %reduce-scatter.11.cloned.1.call-done = bf16[128,2,2048]{2,0,1:T(8,128)(2,1)} async-done(((bf16[2048,2,2048]{2,0,1:T(8,128)(2,1)}), bf16[128,2,2048]{2,0,1:T(8,128)(2,1)}) %reduce-scatter.11.cloned.1.call-update) | async-done | bytes 1048592 | tf_op jit(solution)/shard_map/reduce_scatter | solution.py:191
  (419 shorter events, 436.5 us)
Async XLA Ops:
  8.0 137.2 %copy-start = (bf16[2048,256]{1,0:T(8,128)(2,1)S(1)}, bf16[2048,256]{1,0:T(8,128)(2,1)}, u32[]{:S(2)}) copy-start(bf16[2048,256]{1,0:T(8,128)(2,1)} %param.21) | copy-start | bytes 3145732
  8.0 658.2 %all-reduce.29.cloned.1.call-start = ((), (), s32[]{:S(2)}) async-start(), calls=%async_computation.4 | async-start | bytes 8388608 | tf_op jit(solution)/shard_map/psum | solution.py:155
  8.8 51.4 %copy-start.79 = (s32[8]{0:T(128)}, s32[8]{0:T(128)S(1)}, u32[]{:S(2)}) copy-start(s32[8]{0:T(128)S(1)} %broadcast_maximum_fusion) | copy-start | bytes 100
  9.5 139.9 %copy-start.76 = (pred[8]{0:T(512)(128)(4,1)}, pred[8]{0:T(512)(128)(4,1)S(1)}, u32[]{:S(2)}) copy-start(pred[8]{0:T(512)(128)(4,1)S(1)} %get-tuple-element.411) | copy-start | bytes 28
  12.6 32.9 %copy-start.58 = (f32[1024]{0:T(1024)}, f32[1024]{0:T(1024)S(1)}, u32[]{:S(2)}) copy-start(f32[1024]{0:T(1024)S(1)} %add_rsqrt_fusion.1) | copy-start | bytes 12292
  12.6 32.8 %copy-start.60 = (f32[5,2048]{1,0:T(8,128)S(1)}, f32[5,2048]{1,0:T(8,128)}, u32[]{:S(2)}) copy-start(f32[5,2048]{1,0:T(8,128)} %param.23) | copy-start | bytes 122884
  12.6 32.9 %copy-start.6 = (bf16[1024,2048]{1,0:T(8,128)(2,1)S(1)}, bf16[1024,2048]{1,0:T(8,128)(2,1)}, u32[]{:S(2)}) copy-start(bf16[1024,2048]{1,0:T(8,128)(2,1)} %param.18) | copy-start | bytes 12582916
  12.6 32.9 %copy-start.48 = (f32[2048]{0:T(1024)S(1)}, f32[2048]{0:T(1024)}, u32[]{:S(2)}) copy-start(f32[2048]{0:T(1024)} %param.19) | copy-start | bytes 24580
  93.9 35.0 %copy-start.51 = (s32[8]{0:T(128)S(1)}, s32[8]{0:T(128)}, u32[]{:S(2)}) copy-start(s32[8]{0:T(128)} %param.31) | copy-start | bytes 100
  128.8 32.9 %copy-start.34 = (f32[8,8]{0,1:T(8,128)}, f32[8,8]{0,1:T(8,128)S(1)}, u32[]{:S(2)}) copy-start(f32[8,8]{0,1:T(8,128)S(1)} %fusion.143) | copy-start | bytes 772
  289.8 37.3 %copy-start.61 = (f32[1024]{0:T(1024)}, f32[1024]{0:T(1024)S(1)}, u32[]{:S(2)}) copy-start(f32[1024]{0:T(1024)S(1)} %add_rsqrt_fusion) | copy-start | bytes 12292
  305.2 441.2 %reduce-scatter.9.cloned.1.call-start = ((), (), s32[]{:S(2)}) async-start(), calls=%async_computation.5 | async-start | bytes 6291456 | tf_op jit(solution)/shard_map/reduce_scatter | solution.py:181
  532.1 40.7 %copy-start.10 = (f32[8,128,32]{2,0,1:T(8,128)S(1)}, f32[8,128,32]{2,0,1:T(8,128)}, u32[]{:S(2)}) copy-start(f32[8,128,32]{2,0,1:T(8,128)} %copy-done.9) | copy-start | bytes 393220
  532.1 43.3 %copy-start.13 = (f32[8,128,32]{2,0,1:T(8,128)S(1)}, f32[8,128,32]{2,0,1:T(8,128)}, u32[]{:S(2)}) copy-start(f32[8,128,32]{2,0,1:T(8,128)} %copy.149) | copy-start | bytes 393220
  690.3 164.1 %reduce-scatter.13.cloned.1.call-start = ((), (), s32[]{:S(2)}) async-start(), calls=%async_computation.9 | async-start | bytes 557056
  694.4 222.4 %reduce-scatter.15.cloned.1.call-start = ((), (), s32[]{:S(2)}) async-start(), calls=%async_computation.10 | async-start | bytes 8912896
  722.2 253.4 %all-gather.2.cloned.1.call-start = ((), (), s32[]{:S(2)}) async-start(), calls=%async_computation.6 | async-start | bytes 6291456 | tf_op jit(solution)/shard_map/all_gather | solution.py:189
  755.8 402.9 %reduce-scatter.11.cloned.1.call-start = ((), (), s32[]{:S(2)}) async-start(), calls=%async_computation.7 | async-start | bytes 17825792 | tf_op jit(solution)/shard_map/reduce_scatter | solution.py:191
  785.4 69.0 %copy-start.81 = (f32[256]{0:T(256)S(1)}, f32[256]{0:T(256)}, u32[]{:S(2)}) copy-start(f32[256]{0:T(256)} %get-tuple-element.326) | copy-start | bytes 3076
  785.4 69.0 %copy-start.82 = (f32[256]{0:T(256)S(1)}, f32[256]{0:T(256)}, u32[]{:S(2)}) copy-start(f32[256]{0:T(256)} %get-tuple-element.327) | copy-start | bytes 3076
  785.4 69.0 %copy-start.83 = (f32[256]{0:T(256)S(1)}, f32[256]{0:T(256)}, u32[]{:S(2)}) copy-start(f32[256]{0:T(256)} %get-tuple-element.328) | copy-start | bytes 3076
  785.4 69.0 %copy-start.84 = (f32[256]{0:T(256)S(1)}, f32[256]{0:T(256)}, u32[]{:S(2)}) copy-start(f32[256]{0:T(256)} %get-tuple-element.329) | copy-start | bytes 3076
  785.4 69.0 %copy-start.85 = (f32[256]{0:T(256)S(1)}, f32[256]{0:T(256)}, u32[]{:S(2)}) copy-start(f32[256]{0:T(256)} %get-tuple-element.330) | copy-start | bytes 3076
  785.4 376.9 %all-reduce.31.cloned.1.call-start = ((), (), s32[]{:S(2)}) async-start(), calls=%async_computation.8 | async-start | bytes 4194304 | tf_op jit(solution)/shard_map/psum | solution.py:204
  (81 other events, 998.9 us)
Sparse Core Ops, SparseCore 0:
  305.3 109.7 all-reduce.28
  690.4 55.9 reduce-scatter.8
  750.5 56.5 reduce-scatter.12
  811.6 105.2 reduce-scatter.14
  918.9 56.6 all-gather.1
  980.1 178.5 reduce-scatter.10
Sparse Core Ops, SparseCore 1:
  792.7 204.7 all-reduce.30
where the time goes:
time: 1190 us; the launch traced here: 1180 us
  matrix products  397 us (33%)
  waiting for transfers between devices  279 us (23%)
  other arithmetic  188 us (16%)
  local copies, waits for them, and re-layouts  181 us (15%)
  blocking collectives  113 us (9%)
  between operations  17.5 us (1%)
    reduce_scatter x1, waiting for transfers between devices, local(): lax.psum_scatter(w_zx_part.astype(jnp.bfloat16), 'dp', scatter_dimension=...  183 us
    dot_general x3, matrix products, ssd_mix(): within = jnp.einsum('bijh,bjhp->bihp', weights, x_blocks, precision=highest)  74.5 us
    dot_general x5, matrix products, over_columns(): lax.dot_general(left, right, (((1,), (1,)), ((), ())), preferred_element_...  65.7 us
    psum x1, blocking collectives, local(): lax.psum((conv_x_part, dt_bias_part, a_log_part, d_skip_part, gate_gain_p...  63.7 us
    all_gather x1, waiting for transfers between devices, local(): lax.all_gather(d_input.astype(jnp.bfloat16), 'tensor', axis=0, tiled=True)  56.4 us
    dot_general x5, matrix products, over_tokens(): lax.dot_general(left, right, (((0,), (0,)), ((), ())), preferred_element_...  45.6 us
    dot_general x3, matrix products, ssd_mix(): jnp.einsum('hba,ahpn->bhpn', paths, local_states, precision=highest)  44.6 us
    unnamed x209, local copies, waits for them, and re-layouts  44.2 us
  transfers between devices with their start and end apart: 7, of which 4 were waited for; matrix products, arithmetic and copies ran while one was open for 38% of the time, Pallas kernels for 0%

commit v1 on v0

--- a/solution.py
+++ b/solution.py
@@ -5,6 +5,18 @@
 
 epsilon = 1e-05
 highest = lax.Precision.HIGHEST
+
+
+def gather_by_bits(x, axis, dim):
+    ways, here, hop = (lax.axis_size(axis), lax.axis_index(axis), x.shape[dim])
+    line, have = (x, 1)
+    while have < ways:
+        line = jnp.concatenate(
+            [line, lax.ppermute(line, axis, [(d, (d - have) % ways) for d in range(ways)])],
+            axis=dim,
+        )
+        have = 2 * have
+    return jnp.roll(line, here * hop, axis=dim)
 
 
 def conv_path(inputs, kernel, parent):
@@ -186,7 +198,7 @@
     gained = d_rows * norm_gain
     spread = rms_rows * rms_rows * rms_rows * jnp.sum(gained * x_rows, axis=-1) / features
     d_input = cot_rows + rms_rows[:, None] * gained - x_rows * spread[:, None]
-    input_grad = lax.all_gather(d_input.astype(jnp.bfloat16), "tensor", axis=0, tiled=True)
+    input_grad = gather_by_bits(d_input.astype(jnp.bfloat16), "tensor", 0)
     w_zx_grad, w_dt_grad, w_out_grad = (
         lax.psum_scatter(
             w_zx_part.astype(jnp.bfloat16), "dp", scatter_dimension=0, tiled=True

time: 1190 us -> 1130 us (0.950)
  waiting for transfers between devices: 279 us -> 212 us
    all_gather x1 -> x0, waiting for transfers between devices: 56.4 us -> none  [local(): lax.all_gather(d_input.astype(jnp.bfloat16), 'tensor', axis=0, tiled=True)]
    unnamed x9 -> x8, waiting for transfers between devices: 22.1 us -> 43 us
    reduce_scatter x1, waiting for transfers between devices: 17.5 us -> 0.01 us  [local(): lax.psum_scatter(d_normed.astype(jnp.bfloat16), 'tensor', scatter_dimensi...]
    reduce_scatter x1, waiting for transfers between devices: 183 us -> 169 us  [local(): lax.psum_scatter(w_zx_part.astype(jnp.bfloat16), 'dp', scatter_dimension=...]
    unnamed x209 -> x212, local copies, waits for them, and re-layouts: 44.2 us -> 41.7 us
  transfers between devices with their start and end apart: 7 -> 7, of which waited for: 4 -> 2; matrix products, arithmetic and copies ran while one was open for 38% -> 41% of each run, Pallas kernels for 0% -> 0%
where the time goes in v1:
time: 1130 us; the launch traced here: 1110 us
  matrix products  395 us (35%)
  waiting for transfers between devices  212 us (19%)
  other arithmetic  197 us (17%)
  local copies, waits for them, and re-layouts  178 us (16%)
  blocking collectives  113 us (10%)
  between operations  17 us (2%)
    reduce_scatter x1, waiting for transfers between devices, local(): lax.psum_scatter(w_zx_part.astype(jnp.bfloat16), 'dp', scatter_dimension=...  169 us
    dot_general x3, matrix products, ssd_mix(): within = jnp.einsum('bijh,bjhp->bihp', weights, x_blocks, precision=highest)  74.5 us
    dot_general x5, matrix products, over_columns(): lax.dot_general(left, right, (((1,), (1,)), ((), ())), preferred_element_...  66 us
    psum x1, blocking collectives, local(): lax.psum((conv_x_part, dt_bias_part, a_log_part, d_skip_part, gate_gain_p...  62.2 us
    dot_general x3, matrix products, ssd_mix(): jnp.einsum('hba,ahpn->bhpn', paths, local_states, precision=highest)  44.6 us
    dot_general x5, matrix products, over_tokens(): lax.dot_general(left, right, (((0,), (0,)), ((), ())), preferred_element_...  43.2 us
    unnamed x8, waiting for transfers between devices  43 us
    unnamed x212, local copies, waits for them, and re-layouts  41.7 us
  transfers between devices with their start and end apart: 7, of which 2 were waited for; matrix products, arithmetic and copies ran while one was open for 41% of the time, Pallas kernels for 0%

profile of v1, /device:TPU:0, one launch (start us, length us, event | category | flops | bytes accessed | tf_op | source)
XLA Modules:
  0.0 1114.5 jit_solution(8363036324480666307)
XLA Ops:
  12.6 32.8 %fusion.168 = (bf16[2048,1,2048]{2,1,0:T(2,128)(2,1)}, bf16[2048,1,2048]{2,1,0:T(2,128)(2,1)}) fusion(bf16[2048,2,2048]{2,1,0:T(2,128)(2,1)} %param.20), kind=kLoop, calls=%fused_computation.261 | loop fusion | bytes 33554432 | tf_op jit(solution)/shard_map/slice | solution.py:133
  64.3 16.3 %multiply_convert_fusion.1 = (bf16[8,128,2048]{2,1,0:T(8,128)(2,1)}, f32[8,128,2048]{2,1,0:T(8,128)}) fusion(f32[8,128,2048]{2,1,0:T(8,128)} %copy-done.8, f32[2048]{0:T(1024)S(1)} %bitcast.305, f32[8,3,2048]{2,1,0:T(4,128)S(1)} %select_select_fusion, f32[2048]{0:T(1024)S(1)} %bitcast.307, f32[2048]{0:T(1024)S(1)} %bitcast.301, f32[2048]{0:T(1024)S(1)} %bitcast.303, ...), kind=kLoop, calls=%fused_computation.105 | loop fusion | flops 33554432 | bytes 21209088 | tf_op jit(solution)/shard_map/convert_element_type | solution.py:106
  104.8 23.3 %fusion.174 = f32[8,128,32]{2,0,1:T(8,128)S(1)} fusion(f32[8,128,32]{2,0,1:T(8,128)S(1)} %copy.143), kind=kOutput, calls=%fused_computation.267 | output fusion | flops 4161536 | bytes 262144 | tf_op jit(solution)/shard_map/jvp(jit(cumsum))/reduce_window_sum | solution.py:65
  211.2 21.9 %fusion.39 = f32[8,128,32,64]{1,3,2,0:T(8,128)} fusion(f32[8,128,32,64]{1,3,2,0:T(8,128)} %copy.158, f32[8,128,32,64]{1,3,2,0:T(8,128)S(1)} %fusion.69, f32[32]{0:T(128)S(1)} %copy-done.92, f32[8,128,32]{1,2,0:T(8,128)S(1)} %copy.148, f32[8,128,32]{1,2,0:T(8,128)S(1)} %bitcast.298, f32[8,128,32]{1,2,0:T(8,128)S(1)} %copy-done.38, ...), kind=kOutput, calls=%fused_computation.66 | convolution fusion | flops 3250585600 | bytes 30294144 | tf_op jit(solution)/shard_map/jvp(bijh,bjhp->bihp)/dot_general | solution.py:72
  233.2 16.2 %copy.215 = f32[8,128,32,64]{3,2,1,0:T(8,128)} copy(f32[8,128,32,64]{1,3,2,0:T(8,128)} %fusion.39) | data formatting | bytes 16777216 | tf_op jit(solution)/shard_map/jvp()/reshape | solution.py:82
  249.4 14.8 %reshape.284 = f32[1024,2048]{1,0:T(8,128)} reshape(f32[8,128,32,64]{3,2,1,0:T(8,128)} %copy.215) | data formatting | bytes 16777216 | tf_op jit(solution)/shard_map/jvp()/reshape | solution.py:82
  264.2 19.5 %multiply_reduce_fusion.11 = (f32[1024]{0:T(1024)S(1)}, f32[1024,2048]{1,0:T(8,128)}, f32[1024,2048]{1,0:T(8,128)}) fusion(f32[1024,2048]{1,0:T(8,128)} %reshape.284, bf16[1024,2048]{1,0:T(8,128)(2,1)} %copy-done.2, bf16[2048,1,2048]{2,1,0:T(2,128)(2,1)} %get-tuple-element.379), kind=kOutput, calls=%fused_computation.89 | convolution fusion | flops 8604613632 | bytes 37752832 | tf_op jit(solution)/shard_map/dot_general | solution.py:133
  289.6 15.3 %convolution_convert_fusion.1 = bf16[1024,2048]{1,0:T(8,128)(2,1)} fusion(bf16[2048,2048]{1,0:T(8,128)(2,1)} %param.29, f32[1024,2048]{1,0:T(8,128)} %get-tuple-element.373, f32[2048]{0:T(1024)S(1)} %copy-done.75, f32[1024]{0:T(1024)S(1)} %add_rsqrt_fusion), kind=kOutput, calls=%fused_computation.147 | convolution fusion | flops 8598323200 | bytes 20983808 | tf_op jit(solution)/shard_map/dot_general | solution.py:162
  304.9 17.0 %multiply_reduce_fusion.2 = (f32[2048]{0:T(1024)}, f32[1024]{0:T(1024)S(1)}, f32[1024,2048]{1,0:T(8,128)}) fusion(f32[1024,2048]{1,0:T(8,128)} %get-tuple-element.373, f32[1024]{0:T(1024)S(1)} %add_rsqrt_fusion, f32[2048]{0:T(1024)S(1)} %copy-done.75, bf16[1024,2048]{1,0:T(8,128)(2,1)} %param.30, bf16[2048,2048]{1,0:T(8,128)(2,1)} %param.29), kind=kOutput, calls=%fused_computation.74 | convolution fusion | flops 8602514432 | bytes 29384704 | tf_op jit(solution)/shard_map/dot_general | solution.py:100
  326.9 20.5 %multiply_reduce_fusion.3 = (f32[2048]{0:T(1024)}, f32[1024,2048]{1,0:T(8,128)}, bf16[1024,2048]{1,0:T(8,128)(2,1)}) fusion(bf16[1024,2048]{1,0:T(8,128)(2,1)} %bitcast.262, f32[1024,2048]{1,0:T(8,128)} %get-tuple-element.413, f32[1024,2048]{1,0:T(8,128)} %get-tuple-element.373, f32[1024]{0:T(1024)S(1)} %fusion.144, f32[1024,2048]{1,0:T(8,128)} %get-tuple-element.414, ...), kind=kLoop, calls=%fused_computation.75 | loop fusion | flops 41940992 | bytes 50356224 | tf_op jit(solution)/shard_map/transpose(jvp())/reduce_sum | solution.py:81
  391.0 21.4 %fusion.109 = f32[32,8,8]{2,1,0:T(8,128)S(1)} fusion(f32[32,64,128,8]{2,3,1,0:T(8,128)S(1)} %fusion.44, f32[8,32,64,128]{3,2,1,0:T(8,128)S(1)} %bitcast.259), kind=kOutput, calls=%fused_computation.166 | convolution fusion | flops 201326592 | bytes 16785408 | tf_op jit(solution)/shard_map/transpose(jvp(hba,ahpn->bhpn))/dot_general | solution.py:76
  429.5 18.2 %fusion.106 = f32[8,128,128]{2,1,0:T(8,128)S(1)} fusion(f32[8,32,64,128]{3,0,2,1:T(8,128)} %convolution_bitcast_fusion.1, f32[8,128,32]{1,2,0:T(8,128)S(1)} %copy-done.31, bf16[8,128,32,64]{1,0,3,2:T(8,128)(2,1)S(1)} %bitcast.266), kind=kOutput, calls=%fused_computation.163 | convolution fusion | flops 3225419776 | bytes 13238272 | tf_op jit(solution)/shard_map/transpose(jvp(bjh,bjhp,bjn->bhpn))/dot_general | solution.py:74
  447.8 16.0 %fusion.101 = f32[8,128,128]{2,1,0:T(8,128)S(1)} fusion(f32[8,32,64,128]{3,0,2,1:T(8,128)S(1)} %bitcast.257, f32[8,128,32,64]{1,0,3,2:T(8,128)S(1)} %bitcast.252, f32[8,128,32]{1,2,0:T(8,128)S(1)} %copy.148), kind=kOutput, calls=%fused_computation.162 | convolution fusion | flops 3223322624 | bytes 17432576 | tf_op jit(solution)/shard_map/transpose(jvp(bin,bhpn->bihp))/dot_general | solution.py:78
  463.9 28.9 %fusion.28 = (f32[8,128,32]{1,2,0:T(8,128)}, f32[8,128,32]{1,2,0:T(8,128)S(1)}, f32[8,128,32]{1,2,0:T(8,128)}, f32[8,128,128]{2,1,0:T(8,128)S(1)}) fusion(f32[8,128,32]{1,2,0:T(8,128)S(1)} %bitcast.299, f32[8,128,32]{1,2,0:T(8,128)S(1)} %copy-done.39, f32[8,128,128]{2,1,0:T(8,128)S(1)} %copy-done.33, pred[128,128]{1,0:T(8,128)(4,1)S(1)} %copy-done.66, ...), kind=kOutput, calls=%fused_computation.44 | convolution fusion | flops 3283910656 | bytes 14303232 | tf_op jit(solution)/shard_map/transpose(jvp(bijh,bjhp->bihp))/dot_general | solution.py:72
  508.5 23.6 %bitcast_add_fusion = f32[8,128,32,64]{1,3,2,0:T(8,128)} fusion(f32[8,128,32,64]{1,3,2,0:T(8,128)} %fusion.65, f32[8,128,32,64]{1,0,3,2:T(8,128)S(1)} %bitcast.255, f32[32]{0:T(128)S(1)} %copy-done.93, f32[8,128,32]{1,2,0:T(8,128)S(1)} %copy-done.31, f32[8,128,32]{1,2,0:T(8,128)S(1)} %bitcast.300, f32[8,128,32]{1,2,0:T(8,128)S(1)} %copy-done.39, ...), kind=kOutput, calls=%fused_computation.62 | convolution fusion | flops 3250585600 | bytes 34488448 | tf_op jit(solution)/shard_map/transpose(jvp(bijh,bjhp->bihp))/dot_general | solution.py:72
  536.5 36.3 %while.31 = (s32[]{:T(128)}, f32[8,32]{1,0:T(8,128)}, f32[32,8,8]{2,1,0:T(8,128)S(1)}, f32[8,32,8,8]{3,2,1,0:T(8,128)}, s32[8]{0:T(128)}, /*index=5*/f32[8,32]{0...) while((s32[]{:T(128)}, f32[8,32]{1,0:T(8,128)}, f32[32,8,8]{2,1,0:T(8,128)S(1)}, ...), condition=%wide.region_15.16_spmd.clone, body=%wide.region_14.15_spmd.clone.sunk | while | flops 420484 | bytes 210855 | solution.py:51
  590.6 18.6 %multiply_reduce_fusion.6 = (f32[2048]{0:T(1024)}, f32[2048]{0:T(1024)}, f32[2048]{0:T(1024)}, f32[2048]{0:T(1024)}, f32[2048]{0:T(1024)}, /*index=5*/f32[8,128,2048]{2,1,0:T(8,128)S(1)}) fusion(f32[8,128,2048]{2,1,0:T(8,128)} %copy-done.8, f32[8,3,2048]{2,1,0:T(4,128)S(1)} %copy-done.22, f32[8,128,2048]{2,1,0:T(8,128)} %get-tuple-element.377, ...), kind=kLoop, calls=%fused_computation.78 | loop fusion | flops 44029952 | bytes 33792000 | tf_op jit(solution)/shard_map/transpose(jvp())/reduce_sum | solution.py:34
  650.6 15.9 %fusion.90 = f32[1024,2048]{1,0:T(8,128)} fusion(bf16[1024,2048]{1,0:T(8,128)(2,1)S(1)} %copy-done.16, bf16[2048,1,2048]{2,1,0:T(2,128)(2,1)} %get-tuple-element.379), kind=kOutput, calls=%fused_computation.149 | convolution fusion | flops 8589934592 | bytes 20971520 | tf_op jit(solution)/shard_map/dot_general | solution.py:100
  666.5 24.1 %multiply_reduce_fusion.8 = (f32[2048]{0:T(1024)S(1)}, bf16[1024,2048]{1,0:T(8,128)(2,1)}, bf16[1024,2048]{1,0:T(8,128)(2,1)}) fusion(bf16[1024,2048]{1,0:T(8,128)(2,1)} %param.18, f32[1024]{0:T(1024)S(1)} %copy-done.61, bf16[1024,2048]{1,0:T(8,128)(2,1)} %all-reduce.29.cloned.1.call-done, f32[1024,2048]{1,0:T(8,128)} %fusion.141, ...), kind=kOutput, calls=%fused_computation.82 | convolution fusion | flops 8613001216 | bytes 54538240 | tf_op jit(solution)/shard_map/dot_general | solution.py:100
  694.8 15.2 %convolution_convert_fusion = bf16[2048,2048]{1,0:T(8,128)(2,1)} fusion(bf16[1024,2048]{1,0:T(8,128)(2,1)} %param.30, f32[1024,2048]{1,0:T(8,128)} %get-tuple-element.373, f32[2048]{0:T(1024)S(1)} %copy-done.76, f32[1024]{0:T(1024)S(1)} %copy-done.64), kind=kOutput, calls=%fused_computation.129 | convolution fusion | flops 8600420352 | bytes 20983808 | tf_op jit(solution)/shard_map/dot_general | solution.py:94
  772.0 62.2 %all-reduce.25 = (f32[5,2048]{1,0:T(8,128)}, f32[32]{0:T(128)}, f32[32]{0:T(128)}, f32[32]{0:T(128)}, f32[2048]{0:T(1024)}) all-reduce(f32[5,2048]{1,0:T(8,128)S(1)} %pad_add_fusion.3, f32[32]{0:T(128)S(1)} %get-tuple-element.364, f32[32]{0:T(128)S(1)} %negate_multiply_fusion, ...), channel_id=1, replica_groups=mesh['dp'=16,'tensor'=2] {'dp'}, use_global_device_ids=true, to_apply=%region_32.33 | all-reduce | flops 12384 | bytes 99072 | tf_op jit(solution)/shard_map/psum | solution.py:213
  835.7 39.8 %all-reduce.24 = (f32[2048]{0:T(1024)}, f32[5,256]{1,0:T(8,128)}) all-reduce(f32[2048]{0:T(1024)S(1)} %get-tuple-element.381, f32[5,256]{1,0:T(8,128)S(1)} %pad_add_fusion.4), channel_id=1, replica_groups=mesh['dp'=16,'tensor'=2] {'dp','tensor'}, use_global_device_ids=true, to_apply=%region_23.24 | all-reduce | flops 3328 | bytes 26624 | tf_op jit(solution)/shard_map/psum | solution.py:216
  875.5 42.9 %reduce-scatter.15.cloned.1.call-done = bf16[128,2048]{1,0:T(8,128)(2,1)} async-done(((bf16[2048,2048]{1,0:T(8,128)(2,1)}), bf16[128,2048]{1,0:T(8,128)(2,1)}) %reduce-scatter.15.cloned.1.call-update) | async-done | bytes 524304
  931.9 168.6 %reduce-scatter.11.cloned.1.call-done = bf16[128,2,2048]{2,0,1:T(8,128)(2,1)} async-done(((bf16[2048,2,2048]{2,0,1:T(8,128)(2,1)}), bf16[128,2,2048]{2,0,1:T(8,128)(2,1)}) %reduce-scatter.11.cloned.1.call-update) | async-done | bytes 1048592 | tf_op jit(solution)/shard_map/reduce_scatter | solution.py:203
  (422 shorter events, 413.0 us)
Async XLA Ops:
  8.0 136.9 %copy-start = (bf16[2048,256]{1,0:T(8,128)(2,1)S(1)}, bf16[2048,256]{1,0:T(8,128)(2,1)}, u32[]{:S(2)}) copy-start(bf16[2048,256]{1,0:T(8,128)(2,1)} %param.21) | copy-start | bytes 3145732
  8.0 658.5 %all-reduce.29.cloned.1.call-start = ((), (), s32[]{:S(2)}) async-start(), calls=%async_computation.4 | async-start | bytes 8388608 | tf_op jit(solution)/shard_map/psum | solution.py:167
  8.8 51.4 %copy-start.81 = (s32[8]{0:T(128)}, s32[8]{0:T(128)S(1)}, u32[]{:S(2)}) copy-start(s32[8]{0:T(128)S(1)} %broadcast_maximum_fusion) | copy-start | bytes 100
  9.5 139.6 %copy-start.78 = (pred[8]{0:T(512)(128)(4,1)}, pred[8]{0:T(512)(128)(4,1)S(1)}, u32[]{:S(2)}) copy-start(pred[8]{0:T(512)(128)(4,1)S(1)} %get-tuple-element.411) | copy-start | bytes 28
  12.6 32.9 %copy-start.60 = (f32[1024]{0:T(1024)}, f32[1024]{0:T(1024)S(1)}, u32[]{:S(2)}) copy-start(f32[1024]{0:T(1024)S(1)} %add_rsqrt_fusion.1) | copy-start | bytes 12292
  12.6 32.8 %copy-start.62 = (f32[5,2048]{1,0:T(8,128)S(1)}, f32[5,2048]{1,0:T(8,128)}, u32[]{:S(2)}) copy-start(f32[5,2048]{1,0:T(8,128)} %param.23) | copy-start | bytes 122884
  12.6 32.9 %copy-start.7 = (bf16[1024,2048]{1,0:T(8,128)(2,1)S(1)}, bf16[1024,2048]{1,0:T(8,128)(2,1)}, u32[]{:S(2)}) copy-start(bf16[1024,2048]{1,0:T(8,128)(2,1)} %param.18) | copy-start | bytes 12582916
  12.6 32.9 %copy-start.50 = (f32[2048]{0:T(1024)S(1)}, f32[2048]{0:T(1024)}, u32[]{:S(2)}) copy-start(f32[2048]{0:T(1024)} %param.19) | copy-start | bytes 24580
  93.9 35.0 %copy-start.53 = (s32[8]{0:T(128)S(1)}, s32[8]{0:T(128)}, u32[]{:S(2)}) copy-start(s32[8]{0:T(128)} %param.31) | copy-start | bytes 100
  128.8 32.6 %copy-start.36 = (f32[8,8]{0,1:T(8,128)}, f32[8,8]{0,1:T(8,128)S(1)}, u32[]{:S(2)}) copy-start(f32[8,8]{0,1:T(8,128)S(1)} %fusion.146) | copy-start | bytes 772
  289.6 37.4 %copy-start.63 = (f32[1024]{0:T(1024)}, f32[1024]{0:T(1024)S(1)}, u32[]{:S(2)}) copy-start(f32[1024]{0:T(1024)S(1)} %add_rsqrt_fusion) | copy-start | bytes 12292
  304.9 453.5 %reduce-scatter.9.cloned.1.call-start = ((), (), s32[]{:S(2)}) async-start(), calls=%async_computation.5 | async-start | bytes 6291456 | tf_op jit(solution)/shard_map/reduce_scatter | solution.py:193
  532.1 40.7 %copy-start.11 = (f32[8,128,32]{2,0,1:T(8,128)S(1)}, f32[8,128,32]{2,0,1:T(8,128)}, u32[]{:S(2)}) copy-start(f32[8,128,32]{2,0,1:T(8,128)} %copy-done.10) | copy-start | bytes 393220
  532.1 43.3 %copy-start.14 = (f32[8,128,32]{2,0,1:T(8,128)S(1)}, f32[8,128,32]{2,0,1:T(8,128)}, u32[]{:S(2)}) copy-start(f32[8,128,32]{2,0,1:T(8,128)} %copy.149) | copy-start | bytes 393220
  690.6 143.6 %reduce-scatter.13.cloned.1.call-start = ((), (), s32[]{:S(2)}) async-start(), calls=%async_computation.8 | async-start | bytes 557056
  694.7 223.6 %reduce-scatter.15.cloned.1.call-start = ((), (), s32[]{:S(2)}) async-start(), calls=%async_computation.9 | async-start | bytes 8912896
  722.4 378.1 %reduce-scatter.11.cloned.1.call-start = ((), (), s32[]{:S(2)}) async-start(), calls=%async_computation.6 | async-start | bytes 17825792 | tf_op jit(solution)/shard_map/reduce_scatter | solution.py:203
  751.6 352.5 %all-reduce.31.cloned.1.call-start = ((), (), s32[]{:S(2)}) async-start(), calls=%async_computation.7 | async-start | bytes 4194304 | tf_op jit(solution)/shard_map/psum | solution.py:216
  762.2 71.9 %copy-start.83 = (f32[256]{0:T(256)S(1)}, f32[256]{0:T(256)}, u32[]{:S(2)}) copy-start(f32[256]{0:T(256)} %get-tuple-element.326) | copy-start | bytes 3076
  762.2 71.9 %copy-start.84 = (f32[256]{0:T(256)S(1)}, f32[256]{0:T(256)}, u32[]{:S(2)}) copy-start(f32[256]{0:T(256)} %get-tuple-element.327) | copy-start | bytes 3076
  762.2 71.9 %copy-start.85 = (f32[256]{0:T(256)S(1)}, f32[256]{0:T(256)}, u32[]{:S(2)}) copy-start(f32[256]{0:T(256)} %get-tuple-element.328) | copy-start | bytes 3076
  762.2 71.9 %copy-start.86 = (f32[256]{0:T(256)S(1)}, f32[256]{0:T(256)}, u32[]{:S(2)}) copy-start(f32[256]{0:T(256)} %get-tuple-element.329) | copy-start | bytes 3076
  762.3 71.9 %copy-start.87 = (f32[256]{0:T(256)S(1)}, f32[256]{0:T(256)}, u32[]{:S(2)}) copy-start(f32[256]{0:T(256)} %get-tuple-element.330) | copy-start | bytes 3076
  766.9 155.6 %collective-permute-start = (bf16[512,2048]{1,0:T(8,128)(2,1)S(1)}, bf16[512,2048]{1,0:T(8,128)(2,1)}, u32[]{:S(2)}, u32[]{:S(2)}) collective-permute-start(bf16[512,2048]{1,0:T(8,128)(2,1)S(1)} %subtract_convert_fusion), channel_id=1, source_target_pairs={{0,1},{1,0},{2,3},{3,2},{4,5},{5,4},{6,7},{7,6},{8,9},{9,8},{10,11... | collective-permute-start | bytes 6291464 | tf_op jit(solution)/shard_map/ppermute | solution.py:15
  (83 other events, 1053.3 us)
Sparse Core Ops, SparseCore 0:
  305.0 109.7 all-reduce.28
  690.7 55.8 reduce-scatter.8
  750.8 56.7 reduce-scatter.12
  812.0 106.2 reduce-scatter.14
  922.9 177.5 reduce-scatter.10
Sparse Core Ops, SparseCore 1:
  771.7 166.6 all-reduce.30
